TPU v7x, 512 devices: a whole 4x8x8 slice. The times are simulated.
512 devices in a mesh: dp: 64 (over y, z_hi, core), expert: 8 (over x, z_lo).
Axes of the slice: x: 4, y: 8, z: 8 (z_hi: 4, z_lo: 2; z = z_hi * 2 + z_lo), core: 2. Of those that a mesh axis runs over, the one named last changes fastest.
Arguments:
- activations: bfloat16 [4096, 4096], P('expert', 'dp'), may hold values from -6 to 6
- out_grad: bfloat16 [4096, 4096], P('expert', 'dp'), may hold values from -6 to 6
- w_in: bfloat16 [8, 4096, 8192], P('expert', None, 'dp'), may hold values from -0.25 to 0.25
- w_out: bfloat16 [8, 8192, 4096], P('expert', 'dp'), may hold values from -0.0625 to 0.0625
- chosen: int32 [8, 256], replicated, may hold values from 0 to 4095, as said below
- gate_scores: float32 [8, 256], P('expert'), may hold values from 0.2 to 1
Outputs:
- w_in_grad: bfloat16 [8, 4096, 8192], P('expert', None, 'dp')
- w_out_grad: bfloat16 [8, 8192, 4096], P('expert', 'dp')
- act_grad: bfloat16 [4096, 4096], P('expert', 'dp')
- gate_grad: float32 [8, 256], P('expert')
Inputs may be any that keep to these rules, and one draw needn't show every extreme that they name: Each row of chosen holds 256 distinct token numbers.
All inputs are finite; a program needn't handle non-finite values.
Results may differ from a plain program's by a relative error of at most 0.0075.
Values may be sent and summed in bfloat16 or wider, within the bound.
No kernel may reach another device: no remote copies, remote signals or barrier semaphores. Data moves between devices by JAX's collectives and lax.ppermute only.
A program may use at most 64 MiB of HBM per device.

v0:
```python
import jax
import jax.numpy as jnp
from jax import lax
from jax.sharding import PartitionSpec as P

GELU_SCALE = 0.7978845608
CUBIC_COEF = 0.044715


def gelu_parts(preact):
    inner = GELU_SCALE * (preact + CUBIC_COEF * preact * preact * preact)
    tanh_part = jnp.tanh(inner)
    gelu_val = 0.5 * preact * (1.0 + tanh_part)
    gelu_slope = 0.5 * (1.0 + tanh_part) + 0.5 * preact * (
        1.0 - tanh_part * tanh_part
    ) * GELU_SCALE * (1.0 + 3.0 * CUBIC_COEF * preact * preact)
    return (gelu_val, gelu_slope)


def contract(left_operand, right_operand, left_axis, right_axis):
    return lax.dot_general(
        left_operand,
        right_operand,
        (((left_axis,), (right_axis,)), ((), ())),
        preferred_element_type=jnp.float32,
    )


def exact_contract(left_operand, right_operand, left_axis, right_axis):
    return lax.dot_general(
        left_operand,
        right_operand,
        (((left_axis,), (right_axis,)), ((), ())),
        precision=lax.Precision.HIGHEST,
        preferred_element_type=jnp.float32,
    )


def input_sum(weight_in, preact_back):
    return lax.psum_scatter(
        contract(weight_in, preact_back, 1, 1), "dp", scatter_dimension=0, tiled=True
    )


def per_device(activations, out_grad, w_in, w_out, chosen, gate_scores):
    expert_id = lax.axis_index("expert")
    experts = lax.axis_size("expert")
    own_rows = activations.shape[0]
    every_act, every_grad = (
        lax.all_gather(activations, "expert", axis=0, tiled=True),
        lax.all_gather(out_grad, "expert", axis=0, tiled=True),
    )
    picked = lax.dynamic_index_in_dim(chosen, expert_id, 0, keepdims=False)
    inputs, upstream = (
        lax.all_gather(jnp.take(every_act, picked, axis=0), "dp", axis=1, tiled=True),
        lax.all_gather(jnp.take(every_grad, picked, axis=0), "dp", axis=1, tiled=True),
    )
    weight_in = w_in[0]
    weight_out = w_out[0]
    scores = gate_scores[0]
    gated_grad = (scores[:, None] * upstream.astype(jnp.float32)).astype(jnp.bfloat16)
    preact = jnp.dot(inputs, weight_in, preferred_element_type=jnp.float32)
    gelu_val, gelu_slope = gelu_parts(preact)
    hidden = gelu_val.astype(jnp.bfloat16)
    raw_back = contract(upstream, weight_out, 1, 1)
    gate_grad = lax.psum(jnp.sum(hidden.astype(jnp.float32) * raw_back, axis=1), "dp")
    hidden_back = contract(gated_grad, weight_out, 1, 1)
    preact_back = (hidden_back * gelu_slope).astype(jnp.bfloat16)
    weight_in_grad = contract(inputs, preact_back, 0, 0).astype(jnp.bfloat16)
    weight_out_grad = contract(hidden, gated_grad, 0, 0).astype(jnp.bfloat16)
    summed = input_sum(weight_in, preact_back)
    accumulated = jnp.zeros((summed.shape[0], own_rows), jnp.float32)
    expert_terms = lax.all_gather(summed[None], "expert", axis=0, tiled=True)
    token_ids = expert_id * own_rows + lax.iota(jnp.int32, own_rows)
    for expert_num in range(experts):
        onehot = (chosen[expert_num][None, :] == token_ids[:, None]).astype(jnp.float32)
        accumulated = accumulated + exact_contract(expert_terms[expert_num], onehot, 1, 1)
    act_grad = accumulated.T.astype(jnp.bfloat16)
    return (weight_in_grad[None], weight_out_grad[None], act_grad, gate_grad[None])


def solution(mesh):
    return jax.shard_map(
        per_device,
        mesh=mesh,
        in_specs=(
            P("expert", "dp"),
            P("expert", "dp"),
            P("expert", None, "dp"),
            P("expert", "dp", None),
            P(),
            P("expert", None),
        ),
        out_specs=(
            P("expert", None, "dp"),
            P("expert", "dp", None),
            P("expert", "dp"),
            P("expert", None),
        ),
        check_vma=False,
    )
```

profile of v0, /device:TPU:16, one launch (start us, length us, event | category | flops | bytes accessed | tf_op | source)
XLA Modules:
  0.0 458.6 jit_solution(974488165680355465)
XLA Ops:
  7.2 0.0 copy-start
  7.2 0.0 all-gather.4.cloned.1.call-start
  7.2 1.0 fusion.50
  8.3 1.0 copy.20
  9.3 1.0 copy.22
  10.2 33.9 %all_gather.17 = bf16[4096,64]{1,0:T(8,128)(2,1)S(1)} all-gather(bf16[512,64]{1,0:T(8,128)(2,1)S(1)} %copy.22), channel_id=1, replica_groups=mesh['dp'=64,'expert'=8] {'expert'}, dimensions={0}, use_global_device_ids=true | all-gather | bytes 589824 | tf_op jit(solution)/shard_map/all_gather | solution.py:51
  44.1 32.9 %all_gather.15 = bf16[4096,64]{1,0:T(8,128)(2,1)S(1)} all-gather(bf16[512,64]{1,0:T(8,128)(2,1)S(1)} %copy.20), channel_id=1, replica_groups=mesh['dp'=64,'expert'=8] {'expert'}, dimensions={0}, use_global_device_ids=true | all-gather | bytes 589824 | tf_op jit(solution)/shard_map/all_gather | solution.py:50
  77.0 0.9 gather_fusion.1
  77.9 0.0 copy-start.3
  77.9 0.9 gather_fusion
  78.8 0.1 broadcast_select_fusion
  78.9 0.0 copy-start.4
  78.9 0.7 copy.21
  79.6 0.0 all-gather.4.cloned.1.call-update
  79.6 0.0 all-gather.6.cloned.1.call-start
  79.7 0.7 copy.23
  80.4 0.0 all-gather.6.cloned.1.call-update
  80.4 0.0 reduce-scatter.4.cloned.1.call-start
  80.4 87.1 %all-gather.4.cloned.1.call-done = bf16[256,4096]{0,1:T(8,128)(2,1)} async-done(((bf16[256,64]{0,1:T(8,128)(2,1)}), bf16[256,4096]{0,1:T(8,128)(2,1)}) %all-gather.4.cloned.1.call-update) | async-done | bytes 2097168 | tf_op jit(solution)/shard_map/all_gather | solution.py:55
  167.5 0.0 copy-done
  167.5 2.3 fusion.8
  169.9 83.2 %all-gather.6.cloned.1.call-done = bf16[256,4096]{0,1:T(8,128)(2,1)} async-done(((bf16[256,64]{0,1:T(8,128)(2,1)}), bf16[256,4096]{0,1:T(8,128)(2,1)}) %all-gather.6.cloned.1.call-update) | async-done | bytes 2097168 | tf_op jit(solution)/shard_map/all_gather | solution.py:56
  253.1 0.0 copy-done.3
  253.1 0.0 copy-done.4
  253.1 2.4 fusion.4
  255.5 2.7 convolution_bitcast_fusion
  258.2 5.6 %copy.35 = f32[4096,256]{1,0:T(8,128)} copy(f32[4096,256]{0,1:T(8,128)} %convolution_bitcast_fusion) | data formatting | bytes 8388608
  263.8 0.0 reduce-scatter.4.cloned.1.call-update
  263.8 0.0 copy-start.1
  263.9 2.8 fusion.6
  266.7 121.3 %psum.7 = f32[1,256]{1,0:T(1,128)} all-reduce(f32[1,256]{1,0:T(1,128)S(1)} %bitcast.45), channel_id=1, replica_groups=mesh['dp'=64,'expert'=8] {'dp'}, use_global_device_ids=true, to_apply=%region_2.4 | all-reduce | flops 256 | bytes 2048 | tf_op jit(solution)/shard_map/psum | solution.py:66
  388.1 0.0 copy-done.1
  388.1 0.0 copy-start.2
  388.1 1.7 fusion
  389.7 0.0 copy-done.2
  389.7 1.8 fusion.1
  391.6 26.1 %reduce-scatter.4.cloned.1.call-done = f32[64,256]{1,0:T(8,128)} async-done(((f32[4096,256]{1,0:T(8,128)}), f32[64,256]{1,0:T(8,128)}) %reduce-scatter.4.cloned.1.call-update) | async-done | bytes 65552 | tf_op jit(solution)/shard_map/reduce_scatter | solution.py:40
  417.7 30.2 %all-gather = f32[512,256]{1,0:T(8,128)S(1)} all-gather(f32[64,256]{1,0:T(8,128)} %reduce-scatter.4.cloned.1.call-done), channel_id=2, replica_groups=mesh['dp'=64,'expert'=8] {'expert'}, dimensions={0}, use_global_device_ids=true | all-gather | bytes 589824 | tf_op jit(solution)/shard_map/all_gather | solution.py:73
  447.9 0.4 fusion.19
  448.3 0.4 convolution_add_fusion.6
  448.8 0.4 convolution_add_fusion.5
  449.2 0.4 convolution_add_fusion.4
  449.7 0.4 convolution_add_fusion.3
  450.1 0.4 convolution_add_fusion.2
  450.6 0.4 convolution_add_fusion.1
  451.0 1.1 fusion.5
  (4 shorter events, 0.0 us)
Async XLA Ops:
  7.2 160.4 %copy-start = (bf16[1,4096,128]{2,1,0:T(8,128)(2,1)S(1)}, bf16[1,4096,128]{2,1,0:T(8,128)(2,1)}, u32[]{:S(2)}) copy-start(bf16[1,4096,128]{2,1,0:T(8,128)(2,1)} %param.10) | copy-start | bytes 3145732
  7.2 160.3 %all-gather.4.cloned.1.call-start = ((), (), s32[]{:S(2)}) async-start(), calls=%async_computation.1 | async-start | bytes 2129920 | tf_op jit(solution)/shard_map/all_gather | solution.py:55
  77.9 175.2 %copy-start.3 = (f32[1,256]{1,0:T(1,128)S(1)}, f32[1,256]{1,0:T(1,128)}, u32[]{:S(2)}) copy-start(f32[1,256]{1,0:T(1,128)} %param.13) | copy-start | bytes 3076
  78.9 174.2 %copy-start.4 = (bf16[1,128,4096]{2,1,0:T(8,128)(2,1)S(1)}, bf16[1,128,4096]{2,1,0:T(8,128)(2,1)}, u32[]{:S(2)}) copy-start(bf16[1,128,4096]{2,1,0:T(8,128)(2,1)} %param.11) | copy-start | bytes 3145732
  79.6 173.5 %all-gather.6.cloned.1.call-start = ((), (), s32[]{:S(2)}) async-start(), calls=%async_computation.2 | async-start | bytes 2129920 | tf_op jit(solution)/shard_map/all_gather | solution.py:56
  80.4 337.3 %reduce-scatter.4.cloned.1.call-start = ((), (), s32[]{:S(2)}) async-start(), calls=%async_computation.3 | async-start | bytes 4259840 | tf_op jit(solution)/shard_map/reduce_scatter | solution.py:40
  263.8 124.2 %copy-start.1 = (bf16[256,4096]{0,1:T(8,128)(2,1)S(1)}, bf16[256,4096]{0,1:T(8,128)(2,1)}, u32[]{:S(2)}) copy-start(bf16[256,4096]{0,1:T(8,128)(2,1)} %all-gather.4.cloned.1.call-done) | copy-start | bytes 6291460
  388.1 1.7 copy-start.2
Sparse Core Ops, SparseCore 0:
  79.7 87.7 all-gather.3
  171.4 81.6 all-gather.5
  264.0 153.6 reduce-scatter.3
where the time goes:
time: 459 us
  blocking collectives  218 us (47%)
  waiting for transfers between devices  196 us (43%)
  matrix products  18 us (4%)
  between operations  13.9 us (3%)
  local copies, waits for them, and re-layouts  11.7 us (3%)
    psum x1, blocking collectives, per_device(): lax.psum(jnp.sum(hidden.astype(jnp.float32) * raw_back, axis=1), 'dp')  121 us
    all_gather x1, waiting for transfers between devices, per_device(): lax.all_gather(jnp.take(every_act, picked, axis=0), 'dp', axis=1, tiled=T...  87.1 us
    all_gather x1, waiting for transfers between devices, per_device(): lax.all_gather(jnp.take(every_grad, picked, axis=0), 'dp', axis=1, tiled=...  83.2 us
    all_gather x1, blocking collectives, per_device(): lax.all_gather(out_grad, 'expert', axis=0, tiled=True)  33.9 us
    all_gather x1, blocking collectives, per_device(): lax.all_gather(activations, 'expert', axis=0, tiled=True)  32.9 us
    all_gather x1, blocking collectives, per_device(): expert_terms = lax.all_gather(summed[None], 'expert', axis=0, tiled=True)  30.2 us
    reduce_scatter x1, waiting for transfers between devices, input_sum(): lax.psum_scatter(contract(weight_in, preact_back, 1, 1), 'dp', scatter_di...  26.1 us
    dot_general x5, matrix products, contract(): lax.dot_general(left_operand, right_operand, (((left_axis,), (right_axis,...  11.5 us
  transfers between devices with their start and end apart: 3, of which 3 were waited for; matrix products, arithmetic and copies ran while one was open for 2% of the time, Pallas kernels for 0%

commit v1 on v0

--- a/solution.py
+++ b/solution.py
@@ -70,7 +70,9 @@
     weight_out_grad = contract(hidden, gated_grad, 0, 0).astype(jnp.bfloat16)
     summed = input_sum(weight_in, preact_back)
     accumulated = jnp.zeros((summed.shape[0], own_rows), jnp.float32)
-    expert_terms = lax.all_gather(summed[None], "expert", axis=0, tiled=True)
+    expert_terms = jnp.concatenate(
+        lax.all_to_all(jnp.stack([summed[None]] * lax.axis_size("expert")), "expert", 0, 0), axis=0
+    )
     token_ids = expert_id * own_rows + lax.iota(jnp.int32, own_rows)
     for expert_num in range(experts):
         onehot = (chosen[expert_num][None, :] == token_ids[:, None]).astype(jnp.float32)

time: 459 us -> 589 us (1.28)
  the two profiles are of different devices: /device:TPU:16 before, /device:TPU:3 now
where the time goes in v1:
time: 589 us; the launch traced here: 588 us
  waiting for transfers between devices  334 us (57%)
  blocking collectives  198 us (34%)
  matrix products  24.5 us (4%)
  between operations  13.8 us (2%)
  local copies, waits for them, and re-layouts  13.4 us (2%)
    reduce_scatter x1, waiting for transfers between devices, input_sum(): lax.psum_scatter(contract(weight_in, preact_back, 1, 1), 'dp', scatter_di...  149 us
    psum x1, blocking collectives, per_device(): lax.psum(jnp.sum(hidden.astype(jnp.float32) * raw_back, axis=1), 'dp')  145 us
    all_gather x1, waiting for transfers between devices, per_device(): lax.all_gather(jnp.take(every_act, picked, axis=0), 'dp', axis=1, tiled=T...  102 us
    all_gather x1, waiting for transfers between devices, per_device(): lax.all_gather(jnp.take(every_grad, picked, axis=0), 'dp', axis=1, tiled=...  83.2 us
    all_gather x1, blocking collectives, per_device(): lax.all_gather(activations, 'expert', axis=0, tiled=True)  27.1 us
    all_gather x1, blocking collectives, per_device(): lax.all_gather(out_grad, 'expert', axis=0, tiled=True)  25.9 us
  transfers between devices with their start and end apart: 4, of which 3 were waited for; matrix products, arithmetic and copies ran while one was open for 2% of the time, Pallas kernels for 0%

profile of v1, /device:TPU:3, one launch (start us, length us, event | category | flops | bytes accessed | tf_op | source)
XLA Modules:
  0.0 588.1 jit_solution(3349319585533620086)
XLA Ops:
  7.2 0.0 copy-start
  7.2 0.0 all-gather.3.cloned.1.call-start
  7.2 1.0 fusion.42
  8.3 1.0 copy.21
  9.3 1.0 copy.23
  10.2 25.9 %all_gather.14 = bf16[4096,64]{1,0:T(8,128)(2,1)S(1)} all-gather(bf16[512,64]{1,0:T(8,128)(2,1)S(1)} %copy.23), channel_id=1, replica_groups=mesh['dp'=64,'expert'=8] {'expert'}, dimensions={0}, use_global_device_ids=true | all-gather | bytes 589824 | tf_op jit(solution)/shard_map/all_gather | solution.py:51
  36.1 27.1 %all_gather.12 = bf16[4096,64]{1,0:T(8,128)(2,1)S(1)} all-gather(bf16[512,64]{1,0:T(8,128)(2,1)S(1)} %copy.21), channel_id=1, replica_groups=mesh['dp'=64,'expert'=8] {'expert'}, dimensions={0}, use_global_device_ids=true | all-gather | bytes 589824 | tf_op jit(solution)/shard_map/all_gather | solution.py:50
  63.2 0.9 gather_fusion.1
  64.1 0.0 copy-start.3
  64.1 0.9 gather_fusion
  64.9 0.0 copy-start.4
  64.9 0.1 broadcast_select_fusion
  65.0 0.7 copy.22
  65.8 0.0 all-gather.3.cloned.1.call-update
  65.8 0.0 all-gather.5.cloned.1.call-start
  65.8 0.7 copy.24
  66.5 0.0 all-gather.5.cloned.1.call-update
  66.6 0.0 reduce-scatter.4.cloned.1.call-start
  66.6 101.6 %all-gather.3.cloned.1.call-done = bf16[256,4096]{0,1:T(8,128)(2,1)} async-done(((bf16[256,64]{0,1:T(8,128)(2,1)}), bf16[256,4096]{0,1:T(8,128)(2,1)}) %all-gather.3.cloned.1.call-update) | async-done | bytes 2097168 | tf_op jit(solution)/shard_map/all_gather | solution.py:55
  168.2 0.0 copy-done
  168.2 2.3 fusion.8
  170.5 83.2 %all-gather.5.cloned.1.call-done = bf16[256,4096]{0,1:T(8,128)(2,1)} async-done(((bf16[256,64]{0,1:T(8,128)(2,1)}), bf16[256,4096]{0,1:T(8,128)(2,1)}) %all-gather.5.cloned.1.call-update) | async-done | bytes 2097168 | tf_op jit(solution)/shard_map/all_gather | solution.py:56
  253.8 0.0 copy-done.3
  253.8 0.0 copy-done.4
  253.8 2.4 fusion.4
  256.1 2.7 convolution_bitcast_fusion
  258.8 5.6 copy.36
  264.4 0.0 reduce-scatter.4.cloned.1.call-update
  264.5 148.9 %reduce-scatter.4.cloned.1.call-done = f32[64,256]{1,0:T(8,128)} async-done(((f32[4096,256]{1,0:T(8,128)}), f32[64,256]{1,0:T(8,128)}) %reduce-scatter.4.cloned.1.call-update) | async-done | bytes 65552 | tf_op jit(solution)/shard_map/reduce_scatter | solution.py:40
  413.4 1.7 stack.3
  415.1 0.0 copy-start.1
  415.1 4.6 all-to-all-start
  419.6 2.7 fusion.6
  422.3 144.9 %psum.7 = f32[1,256]{1,0:T(1,128)} all-reduce(f32[1,256]{1,0:T(1,128)S(1)} %bitcast.69), channel_id=1, replica_groups=mesh['dp'=64,'expert'=8] {'dp'}, use_global_device_ids=true, to_apply=%region_2.4 | all-reduce | flops 256 | bytes 2048 | tf_op jit(solution)/shard_map/psum | solution.py:66
  567.2 0.0 copy-done.1
  567.2 0.0 copy-start.2
  567.2 1.7 fusion
  568.9 0.0 copy-done.2
  568.9 1.8 fusion.1
  570.7 0.0 all-to-all-done
  570.7 1.3 fusion.19
  572.0 1.3 convolution_add_fusion.6
  573.3 1.3 convolution_add_fusion.5
  574.6 1.3 convolution_add_fusion.4
  575.8 1.3 convolution_add_fusion.3
  577.1 1.3 convolution_add_fusion.2
  578.4 1.3 convolution_add_fusion.1
  579.7 1.9 fusion.5
  (4 shorter events, 0.0 us)
Async XLA Ops:
  7.2 161.0 %copy-start = (bf16[1,4096,128]{2,1,0:T(8,128)(2,1)S(1)}, bf16[1,4096,128]{2,1,0:T(8,128)(2,1)}, u32[]{:S(2)}) copy-start(bf16[1,4096,128]{2,1,0:T(8,128)(2,1)} %param.10) | copy-start | bytes 3145732
  7.2 161.0 %all-gather.3.cloned.1.call-start = ((), (), s32[]{:S(2)}) async-start(), calls=%async_computation.2 | async-start | bytes 2129920 | tf_op jit(solution)/shard_map/all_gather | solution.py:55
  64.1 189.7 %copy-start.3 = (f32[1,256]{1,0:T(1,128)S(1)}, f32[1,256]{1,0:T(1,128)}, u32[]{:S(2)}) copy-start(f32[1,256]{1,0:T(1,128)} %param.13) | copy-start | bytes 3076
  64.9 188.8 %copy-start.4 = (bf16[1,128,4096]{2,1,0:T(8,128)(2,1)S(1)}, bf16[1,128,4096]{2,1,0:T(8,128)(2,1)}, u32[]{:S(2)}) copy-start(bf16[1,128,4096]{2,1,0:T(8,128)(2,1)} %param.11) | copy-start | bytes 3145732
  65.8 188.0 %all-gather.5.cloned.1.call-start = ((), (), s32[]{:S(2)}) async-start(), calls=%async_computation.3 | async-start | bytes 2129920 | tf_op jit(solution)/shard_map/all_gather | solution.py:56
  66.6 346.8 %reduce-scatter.4.cloned.1.call-start = ((), (), s32[]{:S(2)}) async-start(), calls=%async_computation.4 | async-start | bytes 4259840 | tf_op jit(solution)/shard_map/reduce_scatter | solution.py:40
  415.1 152.1 %copy-start.1 = (bf16[256,4096]{0,1:T(8,128)(2,1)S(1)}, bf16[256,4096]{0,1:T(8,128)(2,1)}, u32[]{:S(2)}) copy-start(bf16[256,4096]{0,1:T(8,128)(2,1)} %all-gather.3.cloned.1.call-done) | copy-start | bytes 6291460
  415.1 155.6 %all-to-all-start = ((f32[8,1,64,256]{3,2,1,0:T(8,128)}), f32[8,1,64,256]{3,2,1,0:T(8,128)}, u32[]{:S(2)}, u32[]{:S(2)}) async-start(f32[8,1,64,256]{3,2,1,0:T(8,128)} %stack.3), calls=%async_computation | async-start | bytes 1048576 | tf_op jit(solution)/shard_map/all_to_all | solution.py:74
  567.2 1.7 copy-start.2
Sparse Core Ops, SparseCore 0:
  65.9 102.2 all-gather.2
  172.1 81.6 all-gather.4
  264.6 148.7 reduce-scatter.3
